TPU v7x, 32 devices: a whole 2x2x4 slice. The times are simulated.
32 devices in a mesh: shard: 2 (over y), ctx: 4 (over z), tp: 4 (over x, core).
Axes of the slice: x: 2, y: 2, z: 4, core: 2. Of those that a mesh axis runs over, the one named last changes fastest.
Arguments:
- inputs: bfloat16 [4, 1024, 768], P('shard', ('ctx', 'tp')), may hold values from -6 to 6
- seg_ids: int32 [4, 1024], P('shard', 'ctx'), may hold values from 0 to 7, never falling along the last dimension, each value on 1 to 512 neighbouring positions
- feature_map: float32 [12, 64, 256], P('tp'), may hold values from -6 to 6
- w_query: bfloat16 [768, 768], P(('shard', 'ctx'), 'tp'), may hold values from -0.21875 to 0.21875
- w_key: bfloat16 [768, 768], P(('shard', 'ctx'), 'tp'), may hold values from -0.21875 to 0.21875
- w_value: bfloat16 [768, 768], P(('shard', 'ctx'), 'tp'), may hold values from -0.21875 to 0.21875
- w_out: bfloat16 [768, 768], P('tp', ('shard', 'ctx')), may hold values from -0.875 to 0.875
- gain_attn: float32 [768], replicated, may hold values from 0.5 to 1.5
- shift_attn: float32 [768], replicated, may hold values from -3 to 3
- w_up: bfloat16 [768, 3072], P(('shard', 'ctx'), 'tp'), may hold values from -0.21875 to 0.21875
- bias_up: float32 [3072], P('tp'), may hold values from -3 to 3
- w_down: bfloat16 [3072, 768], P('tp', ('shard', 'ctx')), may hold values from -0.109375 to 0.109375
- bias_down: float32 [768], replicated, may hold values from -3 to 3
- gain_ffn: float32 [768], replicated, may hold values from 0.5 to 1.5
- shift_ffn: float32 [768], replicated, may hold values from -3 to 3
- cotangent: bfloat16 [4, 1024, 768], P('shard', ('ctx', 'tp')), may hold values from -6 to 6
Outputs:
- outputs: bfloat16 [4, 1024, 768], P('shard', ('ctx', 'tp'))
- grad_inputs: bfloat16 [4, 1024, 768], P('shard', ('ctx', 'tp'))
- grad_query: float32 [768, 768], P(('shard', 'ctx'), 'tp')
- grad_key: float32 [768, 768], P(('shard', 'ctx'), 'tp')
- grad_value: float32 [768, 768], P(('shard', 'ctx'), 'tp')
- grad_out: float32 [768, 768], P('tp', ('shard', 'ctx'))
- grad_gain_attn: float32 [768], replicated
- grad_shift_attn: float32 [768], replicated
- grad_up: float32 [768, 3072], P(('shard', 'ctx'), 'tp')
- grad_bias_up: float32 [3072], P('tp')
- grad_down: float32 [3072, 768], P('tp', ('shard', 'ctx'))
- grad_bias_down: float32 [768], replicated
- grad_gain_ffn: float32 [768], replicated
- grad_shift_ffn: float32 [768], replicated
Inputs may be any that keep to these rules, and one draw needn't show every extreme that they name: `seg_ids`: within each sequence the numbers never fall, every number below 8 occurs, and no document has more than 512 tokens.
All inputs are finite; a program needn't handle non-finite values.
Results may differ from a plain program's by a relative error of at most 0.025.
Values may be sent and summed in bfloat16 or wider, within the bound.
A program may use at most 128 MiB of HBM per device.

v0:
```python
import jax
import jax.numpy as jnp
from jax import lax
from jax.sharding import PartitionSpec as P

HEAD_DIM = 64
FEATS = 256
FF = 3072
SEGS = 8
highest = lax.Precision.HIGHEST
root_half = 0.7071067811865476
inv_root_tau = 0.3989422804014327
norm_eps = 1e-05


def gelu_value(upper):
    return upper * 0.5 * (1.0 + lax.erf(upper * root_half))


def gelu_slope(upper):
    return 0.5 * (1.0 + lax.erf(upper * root_half)) + upper * inv_root_tau * jnp.exp(
        -0.5 * upper * upper
    )


def layer_norm(hidden_in, gain_vec, shift_vec):
    mean_val = jnp.mean(hidden_in, -1, keepdims=True)
    centred = hidden_in - mean_val
    inv_std = lax.rsqrt(jnp.mean(centred * centred, -1, keepdims=True) + norm_eps)
    normed = centred * inv_std
    return (normed * gain_vec + shift_vec, normed, inv_std)


def norm_back(grad_in, normed, inv_std, gain_vec):
    scaled = grad_in * gain_vec
    grad_hidden = inv_std * (
        scaled
        - jnp.mean(scaled, -1, keepdims=True)
        - normed * jnp.mean(scaled * normed, -1, keepdims=True)
    )
    return (grad_hidden, jnp.sum(grad_in * normed, (0, 1)), jnp.sum(grad_in, (0, 1)))


def features(projected, omega_local):
    seq_count, ctx_rows, width = projected.shape
    heads_here = omega_local.shape[0]
    scaled = projected.reshape(seq_count, ctx_rows, heads_here, HEAD_DIM) * HEAD_DIM ** (-0.25)
    angles = jnp.einsum("schd,hdm->schm", scaled, omega_local, precision=highest)
    squares = 0.5 * jnp.sum(scaled * scaled, -1, keepdims=True)
    return (jnp.exp(angles - squares) * FEATS ** (-0.5), scaled)


def feature_back(grad_phi, phi_full, scaled, omega_local):
    grad_angle = grad_phi * phi_full
    grad_scaled = jnp.einsum("schm,hdm->schd", grad_angle, omega_local, precision=highest)
    grad_scaled = grad_scaled - scaled * jnp.sum(grad_angle, -1, keepdims=True)
    seq_count, ctx_rows, heads_here, head_width = scaled.shape
    return (grad_scaled * HEAD_DIM ** (-0.25)).reshape(seq_count, ctx_rows, heads_here * head_width)


def spread_rows(mask_low, left):
    ctx_rows, heads_here, feat_count = left.shape
    wide = mask_low[:, None, :, None] * left[:, :, None, :]
    return wide.reshape(ctx_rows, heads_here, -1)


def segment_outer(operands):
    mask_low, left, right = operands
    return jnp.einsum(
        "chx,che->hxe", spread_rows(mask_low, left), right, preferred_element_type=jnp.float32
    )


def segment_apply(operands):
    mask_low, left, table = operands
    return jnp.einsum(
        "chx,hxe->che", spread_rows(mask_low, left), table, preferred_element_type=jnp.float32
    )


def segment_back(operands):
    mask_full, left, table = operands
    ctx_rows, heads_here, width = left.shape
    seg_count = mask_full.shape[1]
    wide = jnp.einsum("che,hxe->chx", left, table, preferred_element_type=jnp.float32)
    wide = wide.reshape(ctx_rows, heads_here, seg_count, -1)
    return jnp.sum(wide * mask_full[:, None, :, None], 2)


def inner_product(left, right):
    return lax.dot_general(
        left, right, (((0,), (0,)), ((), ())), preferred_element_type=jnp.float32
    )


def right_transposed(left, right):
    return lax.dot_general(
        left, right, (((1,), (1,)), ((), ())), preferred_element_type=jnp.float32
    )


def per_device(
    inputs,
    seg_ids,
    feature_map,
    w_query,
    w_key,
    w_value,
    w_out,
    gain_attn,
    shift_attn,
    w_up,
    bias_up,
    w_down,
    bias_down,
    gain_ffn,
    shift_ffn,
    cotangent,
):
    full_query, full_key, full_value, full_up, full_out, full_down = (
        lax.all_gather(w_query, ("shard", "ctx"), axis=0, tiled=True),
        lax.all_gather(w_key, ("shard", "ctx"), axis=0, tiled=True),
        lax.all_gather(w_value, ("shard", "ctx"), axis=0, tiled=True),
        lax.all_gather(w_up, ("shard", "ctx"), axis=0, tiled=True),
        lax.all_gather(w_out, ("shard", "ctx"), axis=1, tiled=True),
        lax.all_gather(w_down, ("shard", "ctx"), axis=1, tiled=True),
    )
    seq_count, row_share, width = inputs.shape
    rows_all = lax.all_gather(inputs, "tp", axis=1, tiled=True)
    ctx_rows = rows_all.shape[1]
    token_count = seq_count * ctx_rows
    flat = rows_all.reshape(token_count, width)
    heads_here = feature_map.shape[0]
    head_cols = heads_here * HEAD_DIM
    query_proj = jnp.dot(flat, full_query, preferred_element_type=jnp.float32).reshape(
        seq_count, ctx_rows, head_cols
    )
    key_proj = jnp.dot(flat, full_key, preferred_element_type=jnp.float32).reshape(
        seq_count, ctx_rows, head_cols
    )
    value_low = jnp.dot(flat, full_value, preferred_element_type=jnp.float32).astype(jnp.bfloat16)
    value_low = value_low.reshape(seq_count, ctx_rows, head_cols)
    value_four = value_low.reshape(seq_count, ctx_rows, heads_here, HEAD_DIM)
    phi_query, scaled_query = features(query_proj, feature_map)
    phi_key, scaled_key = features(key_proj, feature_map)
    phq_low = phi_query.astype(jnp.bfloat16)
    phk_low = phi_key.astype(jnp.bfloat16)
    matches = seg_ids[:, :, None] == jnp.arange(SEGS, dtype=jnp.int32)[None, None, :]
    mask_low = matches.astype(jnp.bfloat16)
    mask_full = matches.astype(jnp.float32)
    kv_part = lax.map(segment_outer, (mask_low, phk_low, value_four))
    z_part = jnp.einsum("scg,schm->shgm", mask_low, phk_low, preferred_element_type=jnp.float32)
    kv_sum, z_sum = lax.psum((kv_part, z_part), "ctx")
    kv_low = kv_sum.astype(jnp.bfloat16)
    numer = lax.map(segment_apply, (mask_low, phq_low, kv_low))
    phq_wide = phq_low.astype(jnp.float32)
    denom = jnp.sum(
        jnp.einsum("schm,shgm->schg", phq_wide, z_sum, precision=highest)
        * mask_full[:, :, None, :],
        -1,
    )
    mixed = numer / denom[..., None]
    mixed_low = mixed.astype(jnp.bfloat16).reshape(seq_count, ctx_rows, head_cols)
    piece = mixed_low
    attn_sum = jnp.swapaxes(
        lax.psum_scatter(
            jnp.einsum("scf,fd->csd", piece, full_out, preferred_element_type=jnp.float32),
            "tp",
            scatter_dimension=0,
            tiled=True,
        ),
        0,
        1,
    )
    first, normed_one, inv_one = layer_norm(
        inputs.astype(jnp.float32) + attn_sum, gain_attn, shift_attn
    )
    first_low = first.astype(jnp.bfloat16)
    first_rows = lax.all_gather(first_low, "tp", axis=1, tiled=True)
    first_flat = first_rows.reshape(token_count, width)
    upper = jnp.dot(first_flat, full_up, preferred_element_type=jnp.float32) + bias_up
    ffn_here = upper.shape[1]
    hidden_low = gelu_value(upper).astype(jnp.bfloat16)
    hidden_three = hidden_low.reshape(seq_count, ctx_rows, ffn_here)
    piece = hidden_three
    branch = jnp.swapaxes(
        lax.psum_scatter(
            jnp.einsum("scf,fd->csd", piece, full_down, preferred_element_type=jnp.float32),
            "tp",
            scatter_dimension=0,
            tiled=True,
        ),
        0,
        1,
    )
    final, normed_two, inv_two = layer_norm(first + branch + bias_down, gain_ffn, shift_ffn)
    outputs = final.astype(jnp.bfloat16)
    full_query, full_key, full_value, full_up, full_out, full_down = (
        lax.all_gather(w_query, ("shard", "ctx"), axis=0, tiled=True),
        lax.all_gather(w_key, ("shard", "ctx"), axis=0, tiled=True),
        lax.all_gather(w_value, ("shard", "ctx"), axis=0, tiled=True),
        lax.all_gather(w_up, ("shard", "ctx"), axis=0, tiled=True),
        lax.all_gather(w_out, ("shard", "ctx"), axis=1, tiled=True),
        lax.all_gather(w_down, ("shard", "ctx"), axis=1, tiled=True),
    )
    grad_final = cotangent.astype(jnp.float32)
    grad_two, grad_gain_ffn, grad_shift_ffn = norm_back(grad_final, normed_two, inv_two, gain_ffn)
    grad_bias_down = jnp.sum(grad_two, (0, 1))
    grad_two_rows = lax.all_gather(grad_two.astype(jnp.bfloat16), "tp", axis=1, tiled=True)
    grad_two_flat = grad_two_rows.reshape(token_count, width)
    grad_hidden = right_transposed(grad_two_flat, full_down)
    grad_upper = (grad_hidden * gelu_slope(upper)).astype(jnp.bfloat16)
    grad_down = inner_product(hidden_low, grad_two_flat)
    grad_up = inner_product(first_flat, grad_upper)
    grad_bias_local = jnp.sum(grad_upper.astype(jnp.float32), 0)
    grad_upper_three = grad_upper.reshape(seq_count, ctx_rows, ffn_here)
    piece = grad_upper_three
    grad_first = grad_two + jnp.swapaxes(
        lax.psum_scatter(
            jnp.einsum("scf,df->csd", piece, full_up, preferred_element_type=jnp.float32),
            "tp",
            scatter_dimension=0,
            tiled=True,
        ),
        0,
        1,
    )
    grad_one, grad_gain_attn, grad_shift_attn = norm_back(
        grad_first, normed_one, inv_one, gain_attn
    )
    grad_one_rows = lax.all_gather(grad_one.astype(jnp.bfloat16), "tp", axis=1, tiled=True)
    grad_one_flat = grad_one_rows.reshape(token_count, width)
    grad_out = inner_product(mixed_low.reshape(token_count, head_cols), grad_one_flat)
    grad_mixed = right_transposed(grad_one_flat, full_out).reshape(
        seq_count, ctx_rows, heads_here, HEAD_DIM
    )
    grad_numer = (grad_mixed / denom[..., None]).astype(jnp.bfloat16)
    grad_denom = -jnp.sum(grad_mixed * mixed, -1) / denom
    kv_grad_part = lax.map(segment_outer, (mask_low, phq_low, grad_numer))
    z_grad_part = jnp.einsum(
        "scg,schm->shgm", mask_full, phq_wide * grad_denom[..., None], precision=highest
    )
    kv_grad, z_grad = (
        lax.psum(kv_grad_part.astype(jnp.bfloat16), "ctx").astype(jnp.float32),
        lax.psum(z_grad_part.astype(jnp.bfloat16), "ctx").astype(jnp.float32),
    )
    kv_grad_low = kv_grad.astype(jnp.bfloat16)
    grad_phq = lax.map(segment_back, (mask_full, grad_numer, kv_low))
    grad_phq = grad_phq + grad_denom[..., None] * jnp.einsum(
        "scg,shgm->schm", mask_full, z_sum, precision=highest
    )
    grad_phk = lax.map(segment_back, (mask_full, value_four, kv_grad_low))
    grad_phk = grad_phk + jnp.einsum("scg,shgm->schm", mask_full, z_grad, precision=highest)
    grad_value_rows = lax.map(segment_apply, (mask_low, phk_low, kv_grad_low)).astype(jnp.bfloat16)
    grad_value_rows = grad_value_rows.reshape(seq_count, ctx_rows, head_cols)
    grad_query_rows = feature_back(grad_phq, phi_query, scaled_query, feature_map).astype(
        jnp.bfloat16
    )
    grad_key_rows = feature_back(grad_phk, phi_key, scaled_key, feature_map).astype(jnp.bfloat16)
    grad_query = inner_product(flat, grad_query_rows.reshape(token_count, head_cols))
    grad_key = inner_product(flat, grad_key_rows.reshape(token_count, head_cols))
    grad_value = inner_product(flat, grad_value_rows.reshape(token_count, head_cols))
    total = jnp.einsum(
        "scf,df->csd", grad_query_rows, full_query, preferred_element_type=jnp.float32
    )
    total = total + jnp.einsum(
        "scf,df->csd", grad_key_rows, full_key, preferred_element_type=jnp.float32
    )
    grad_rows = jnp.swapaxes(
        lax.psum_scatter(
            (
                total
                + jnp.einsum(
                    "scf,df->csd", grad_value_rows, full_value, preferred_element_type=jnp.float32
                )
            ).astype(jnp.bfloat16),
            "tp",
            scatter_dimension=0,
            tiled=True,
        ).astype(jnp.float32),
        0,
        1,
    )
    grad_inputs = (grad_one + grad_rows).astype(jnp.bfloat16)
    grad_query, grad_key, grad_value, grad_up, grad_out, grad_down = (
        lax.psum_scatter(grad_query, ("shard", "ctx"), scatter_dimension=0, tiled=True),
        lax.psum_scatter(grad_key, ("shard", "ctx"), scatter_dimension=0, tiled=True),
        lax.psum_scatter(grad_value, ("shard", "ctx"), scatter_dimension=0, tiled=True),
        lax.psum_scatter(grad_up, ("shard", "ctx"), scatter_dimension=0, tiled=True),
        lax.psum_scatter(grad_out, ("shard", "ctx"), scatter_dimension=1, tiled=True),
        lax.psum_scatter(grad_down, ("shard", "ctx"), scatter_dimension=1, tiled=True),
    )
    tp_index = lax.axis_index("tp")
    padded_bias = lax.dynamic_update_slice(
        jnp.zeros((FF,), jnp.float32), grad_bias_local, (tp_index * ffn_here,)
    )
    grad_gain_attn, grad_shift_attn, grad_gain_ffn, grad_shift_ffn, grad_bias_down, padded_bias = (
        lax.psum(
            (
                grad_gain_attn,
                grad_shift_attn,
                grad_gain_ffn,
                grad_shift_ffn,
                grad_bias_down,
                padded_bias,
            ),
            ("shard", "ctx", "tp"),
        )
    )
    grad_bias_up = lax.dynamic_slice(padded_bias, (tp_index * ffn_here,), (ffn_here,))
    return (
        outputs,
        grad_inputs,
        grad_query,
        grad_key,
        grad_value,
        grad_out,
        grad_gain_attn,
        grad_shift_attn,
        grad_up,
        grad_bias_up,
        grad_down,
        grad_bias_down,
        grad_gain_ffn,
        grad_shift_ffn,
    )


def solution(mesh):
    placed = (
        P("shard", ("ctx", "tp"), None),
        P("shard", "ctx"),
        P("tp", None, None),
        P(("shard", "ctx"), "tp"),
        P(("shard", "ctx"), "tp"),
        P(("shard", "ctx"), "tp"),
        P("tp", ("shard", "ctx")),
        P(),
        P(),
        P(("shard", "ctx"), "tp"),
        P("tp"),
        P("tp", ("shard", "ctx")),
        P(),
        P(),
        P(),
        P("shard", ("ctx", "tp"), None),
    )
    return jax.shard_map(
        per_device,
        mesh=mesh,
        in_specs=placed,
        out_specs=(
            P("shard", ("ctx", "tp"), None),
            P("shard", ("ctx", "tp"), None),
            P(("shard", "ctx"), "tp"),
            P(("shard", "ctx"), "tp"),
            P(("shard", "ctx"), "tp"),
            P("tp", ("shard", "ctx")),
            P(),
            P(),
            P(("shard", "ctx"), "tp"),
            P("tp"),
            P("tp", ("shard", "ctx")),
            P(),
            P(),
            P(),
        ),
        check_vma=False,
    )
```

profile of v0, /device:TPU:0, one launch (start us, length us, event | category | flops | bytes accessed | tf_op | source)
XLA Modules:
  0.0 1010.8 jit_solution(17872332154931087539)
XLA Ops:
  8.1 10.4 %all_gather.36 = bf16[2,256,768]{2,1,0:T(8,128)(2,1)S(1)} all-gather(bf16[2,64,768]{2,1,0:T(8,128)(2,1)} %param.28), channel_id=1, replica_groups=mesh['shard'=2,'ctx'=4,'tp'=4] {'tp'}, dimensions={1}, use_global_device_ids=true | all-gather | bytes 983040 | tf_op jit(solution)/shard_map/all_gather | solution.py:129
  18.5 32.5 %all_gather.37 = bf16[768,192]{1,0:T(8,128)(2,1)S(1)} all-gather(bf16[96,192]{1,0:T(8,128)(2,1)} %param.32), channel_id=1, replica_groups=mesh['shard'=2,'ctx'=4,'tp'=4] {'shard','ctx'}, dimensions={0}, use_global_device_ids=true | all-gather | bytes 331776 | tf_op jit(solution)/shard_map/all_gather | solution.py:122
  56.2 31.6 %all_gather.38 = bf16[768,192]{1,0:T(8,128)(2,1)S(1)} all-gather(bf16[96,192]{1,0:T(8,128)(2,1)S(1)} %copy-done.48), channel_id=1, replica_groups=mesh['shard'=2,'ctx'=4,'tp'=4] {'shard','ctx'}, dimensions={0}, use_global_device_ids=true | all-gather | bytes 331776 | tf_op jit(solution)/shard_map/all_gather | solution.py:123
  92.7 20.8 %while.66 = (s32[]{:T(128)}, f32[2,3,2048,64]{2,3,1,0:T(8,128)}, bf16[2,256,8]{2,1,0:T(8,128)(2,1)S(1)}, bf16[2,256,3,256]{3,1,2,0:T(8,128)(2,1)}, bf16[2,256,3,64]{1,3,2,0:T(8,128)(2,1)}) while((s32[]{:T(128)}, f32[2,3,2048,64]{2,3,1,0:T(8,128)}, bf16[2,256,8]{2,1,0:T(8,128)(2,1)S(1)}, bf16[2,256,3,256]{3,1,2,0:T(8,128)(2,1)}, ...), condition=%wide.region_3.4_spmd.clone, body=%wide.region_2.3_spmd.sunk.clone | while | flops 207618048 | bytes 20427872 | solution.py:151
  95.9 4.2 mul.740
  106.4 4.2 mul.740
  113.6 32.0 %all_gather.39 = bf16[768,192]{1,0:T(8,128)(2,1)S(1)} all-gather(bf16[96,192]{1,0:T(8,128)(2,1)S(1)} %copy-done.49), channel_id=1, replica_groups=mesh['shard'=2,'ctx'=4,'tp'=4] {'shard','ctx'}, dimensions={0}, use_global_device_ids=true | all-gather | bytes 331776 | tf_op jit(solution)/shard_map/all_gather | solution.py:121
  152.0 96.4 %all-reduce.6 = (bf16[2,3,2048,64]{2,3,1,0:T(8,128)(2,1)}, f32[2,3,8,256]{3,2,1,0:T(8,128)S(1)}) all-reduce(f32[2,3,2048,64]{2,3,1,0:T(8,128)} %get-tuple-element.176, f32[2,3,8,256]{3,2,1,0:T(8,128)S(1)} %copy-done.46), channel_id=1, replica_groups=mesh['shard'=2,'ctx'=4,'tp'=4] {'ctx'}, use_global_device_ids=true, to_apply=%region_4.5 | all-reduce | flops 798720 | bytes 4816896 | tf_op jit(solution)/shard_map/psum | solution.py:153
  248.4 19.4 %while.67 = (s32[]{:T(128)}, f32[2,256,3,64]{1,3,2,0:T(8,128)}, bf16[2,3,2048,64]{2,3,1,0:T(8,128)(2,1)}, bf16[2,256,8]{2,1,0:T(8,128)(2,1)S(1)}, bf16[2,256,3,256]{3,1,2,0:T(8,128)(2,1)}) while((s32[]{:T(128)}, f32[2,256,3,64]{1,3,2,0:T(8,128)}, bf16[2,3,2048,64]{2,3,1,0:T(8,128)(2,1)}, bf16[2,256,8]{2,1,0:T(8,128)(2,1)S(1)}, ...), condition=%wide.region_6.7_spmd.clone, body=%wide.region_5.6_spmd.sunk.clone | while | flops 202899456 | bytes 31536224 | solution.py:155
  268.7 31.8 %all_gather.40 = bf16[192,768]{0,1:T(8,128)(2,1)S(1)} all-gather(bf16[192,96]{0,1:T(8,128)(2,1)S(1)} %copy.105), channel_id=1, replica_groups=mesh['shard'=2,'ctx'=4,'tp'=4] {'shard','ctx'}, dimensions={1}, use_global_device_ids=true | all-gather | bytes 331776 | tf_op jit(solution)/shard_map/all_gather | solution.py:125
  305.4 27.2 %reduce-scatter.19.cloned.1.call-done = f32[64,2,768]{2,0,1:T(8,128)} async-done(((f32[256,2,768]{2,0,1:T(8,128)}), f32[64,2,768]{2,0,1:T(8,128)}) %reduce-scatter.19.cloned.1.call-update) | async-done | bytes 393232 | tf_op jit(solution)/shard_map/reduce_scatter | solution.py:166
  334.7 8.0 all_gather.41
  342.7 5.8 all-gather.3.cloned.1.call-done
  351.7 38.5 %all-gather.5.cloned.1.call-done = bf16[768,768]{0,1:T(8,128)(2,1)} async-done(((bf16[768,96]{0,1:T(8,128)(2,1)}), bf16[768,768]{0,1:T(8,128)(2,1)}) %all-gather.5.cloned.1.call-update) | async-done | bytes 1179664 | tf_op jit(solution)/shard_map/all_gather | solution.py:126
  393.6 26.5 %reduce-scatter.21.cloned.1.call-done = f32[64,2,768]{2,0,1:T(8,128)} async-done(((f32[256,2,768]{2,0,1:T(8,128)}), f32[64,2,768]{2,0,1:T(8,128)}) %reduce-scatter.21.cloned.1.call-update) | async-done | bytes 393232 | tf_op jit(solution)/shard_map/reduce_scatter | solution.py:187
  422.0 8.1 all_gather.44
  438.0 25.5 %reduce-scatter.23.cloned.1.call-done = f32[64,2,768]{2,0,1:T(8,128)} async-done(((f32[256,2,768]{2,0,1:T(8,128)}), f32[64,2,768]{2,0,1:T(8,128)}) %reduce-scatter.23.cloned.1.call-update) | async-done | bytes 393232 | tf_op jit(solution)/shard_map/reduce_scatter | solution.py:219
  466.4 8.0 all_gather.45
  476.2 20.0 %while.69 = (s32[]{:T(128)}, bf16[2,3,2048,64]{2,3,1,0:T(8,128)(2,1)}, bf16[2,256,8]{2,1,0:T(8,128)(2,1)S(1)}, bf16[2,256,3,256]{3,1,2,0:T(8,128)(2,1)}, bf16[2,256,3,64]{1,3,2,0:T(8,128)(2,1)}) while((s32[]{:T(128)}, bf16[2,3,2048,64]{2,3,1,0:T(8,128)(2,1)}, bf16[2,256,8]{2,1,0:T(8,128)(2,1)S(1)}, ...), condition=%wide.region_26.27_spmd.clone, body=%wide.region_25.26_spmd.sunk.clone | while | flops 207618048 | bytes 20427872 | solution.py:239
  479.2 4.2 mul.752
  489.2 4.2 mul.752
  497.8 7.0 while.68
  508.3 20.2 %psum.73 = bf16[2,3,8,256]{3,2,1,0:T(8,128)(2,1)S(1)} all-reduce(bf16[2,3,8,256]{3,2,1,0:T(8,128)(2,1)S(1)} %fusion.107), channel_id=1, replica_groups=mesh['shard'=2,'ctx'=4,'tp'=4] {'ctx'}, use_global_device_ids=true, to_apply=%region_31.32 | all-reduce | flops 12288 | bytes 49152 | tf_op jit(solution)/shard_map/psum | solution.py:245
  532.7 33.9 %all-reduce.5.cloned.1.call-done = bf16[2,3,2048,64]{2,3,1,0:T(8,128)(2,1)} async-done(((bf16[2,3,2048,64]{2,3,1,0:T(8,128)(2,1)}), bf16[2,3,2048,64]{2,3,1,0:T(8,128)(2,1)}) %all-reduce.5.cloned.1.call-update) | async-done | bytes 1572880 | tf_op jit(solution)/shard_map/psum | solution.py:244
  568.0 7.5 while.70
  580.4 19.7 %while.71 = (s32[]{:T(128)}, bf16[2,256,3,64]{1,3,2,0:T(8,128)(2,1)}, bf16[2,3,2048,64]{2,3,1,0:T(8,128)(2,1)}, bf16[2,256,8]{2,1,0:T(8,128)(2,1)S(1)}, bf16[2,256,3,256]{3,1,2,0:T(8,128)(2,1)}) while((s32[]{:T(128)}, bf16[2,256,3,64]{1,3,2,0:T(8,128)(2,1)}, bf16[2,3,2048,64]{2,3,1,0:T(8,128)(2,1)}, ...), condition=%wide.region_34.35_spmd.clone, body=%wide.region_33.34_spmd.sunk.clone | while | flops 202899456 | bytes 33109144 | solution.py:254
  616.1 40.8 %all-reduce = (f32[768]{0:T(1024)}, f32[768]{0:T(1024)}, f32[3072]{0:T(1024)S(1)}, f32[768]{0:T(1024)}, f32[768]{0:T(1024)}, /*index=5*/f32[768]{0:T(1024)}) all-reduce(f32[768]{0:T(1024)S(1)} %copy-done.69, f32[768]{0:T(1024)S(1)} %copy-done.68, ...), channel_id=1, replica_groups=mesh['shard'=2,'ctx'=4,'tp'=4] {'shard','ctx','tp'}, use_global_device_ids=true, to_apply=%region_41.42 | all-reduce | flops 6912 | bytes 55296 | tf_op jit(solution)/shard_map/psum | solution.py:298
  661.1 63.8 %reduce-scatter.31.cloned.1.call-done = f32[96,192]{1,0:T(8,128)} async-done(((f32[768,192]{1,0:T(8,128)}), f32[96,192]{1,0:T(8,128)}) %reduce-scatter.31.cloned.1.call-update) | async-done | bytes 73744
  724.9 73.0 %reduce-scatter.29.cloned.1.call-done = f32[768,96]{0,1:T(8,128)} async-done(((f32[768,768]{0,1:T(8,128)}), f32[768,96]{0,1:T(8,128)}) %reduce-scatter.29.cloned.1.call-update) | async-done | bytes 294928 | tf_op jit(solution)/shard_map/reduce_scatter | solution.py:291
  797.9 73.1 %reduce-scatter.27.cloned.1.call-done = f32[96,768]{1,0:T(8,128)} async-done(((f32[768,768]{1,0:T(8,128)}), f32[96,768]{1,0:T(8,128)}) %reduce-scatter.27.cloned.1.call-update) | async-done | bytes 294928 | tf_op jit(solution)/shard_map/reduce_scatter | solution.py:289
  871.0 66.2 %reduce-scatter.33.cloned.1.call-done = f32[96,192]{1,0:T(8,128)} async-done(((f32[768,192]{1,0:T(8,128)}), f32[96,192]{1,0:T(8,128)}) %reduce-scatter.33.cloned.1.call-update) | async-done | bytes 73744
  937.2 66.2 %reduce-scatter.35.cloned.1.call-done = f32[96,192]{1,0:T(8,128)} async-done(((f32[768,192]{1,0:T(8,128)}), f32[96,192]{1,0:T(8,128)}) %reduce-scatter.35.cloned.1.call-update) | async-done | bytes 73744
  (358 shorter events, 157.6 us)
Async XLA Ops:
  8.0 44.3 %copy-start = (f32[3,64,256]{2,1,0:T(8,128)S(1)}, f32[3,64,256]{2,1,0:T(8,128)}, u32[]{:S(2)}) copy-start(f32[3,64,256]{2,1,0:T(8,128)} %param.30) | copy-start | bytes 589828
  8.0 324.6 %reduce-scatter.19.cloned.1.call-start = ((), (), s32[]{:S(2)}) async-start(), calls=%async_computation.10 | async-start | bytes 1966080 | tf_op jit(solution)/shard_map/reduce_scatter | solution.py:166
  18.5 69.3 %copy-start.4 = (bf16[2,256,768]{2,1,0:T(8,128)(2,1)}, bf16[2,256,768]{2,1,0:T(8,128)(2,1)S(1)}, u32[]{:S(2)}) copy-start(bf16[2,256,768]{2,1,0:T(8,128)(2,1)S(1)} %all_gather.36) | copy-start | bytes 2359300
  56.2 33.5 %copy-start.56 = (s32[2,256]{1,0:T(2,128)S(1)}, s32[2,256]{1,0:T(2,128)}, u32[]{:S(2)}) copy-start(s32[2,256]{1,0:T(2,128)} %param.29) | copy-start | bytes 6148
  150.7 97.6 %copy-start.24 = (bf16[2,256,3,256]{1,3,0,2:T(8,128)(2,1)}, bf16[2,256,3,256]{1,3,0,2:T(8,128)(2,1)S(1)}, u32[]{:S(2)}) copy-start(bf16[2,256,3,256]{1,3,0,2:T(8,128)(2,1)S(1)} %get-tuple-element.414) | copy-start | bytes 2359300
  267.8 34.6 %copy-start.45 = (f32[2,256,3,64]{1,3,2,0:T(8,128)S(1)}, f32[2,256,3,64]{1,3,2,0:T(8,128)}, u32[]{:S(2)}) copy-start(f32[2,256,3,64]{1,3,2,0:T(8,128)} %get-tuple-element.177) | copy-start | bytes 1179652
  302.5 30.1 %copy-start.42 = (bf16[2,64,768]{2,1,0:T(8,128)(2,1)S(1)}, bf16[2,64,768]{2,1,0:T(8,128)(2,1)}, u32[]{:S(2)}) copy-start(bf16[2,64,768]{2,1,0:T(8,128)(2,1)} %param.28) | copy-start | bytes 589828
  304.1 30.4 %copy-start.47 = (f32[768]{0:T(1024)S(1)}, f32[768]{0:T(1024)}, u32[]{:S(2)}) copy-start(f32[768]{0:T(1024)} %param.35) | copy-start | bytes 9220
  304.1 30.4 %copy-start.61 = (f32[768]{0:T(1024)S(1)}, f32[768]{0:T(1024)}, u32[]{:S(2)}) copy-start(f32[768]{0:T(1024)} %param.36) | copy-start | bytes 9220
  304.1 44.3 %all-gather.3.cloned.1.call-start = ((), (), s32[]{:S(2)}) async-start(), calls=%async_computation.11 | async-start | bytes 1327104 | tf_op jit(solution)/shard_map/all_gather | solution.py:124
  304.7 85.5 %all-gather.5.cloned.1.call-start = ((), (), s32[]{:S(2)}) async-start(), calls=%async_computation.12 | async-start | bytes 1327104 | tf_op jit(solution)/shard_map/all_gather | solution.py:126
  305.3 114.8 %reduce-scatter.21.cloned.1.call-start = ((), (), s32[]{:S(2)}) async-start(), calls=%async_computation.13 | async-start | bytes 1966080 | tf_op jit(solution)/shard_map/reduce_scatter | solution.py:187
  333.7 132.5 %copy-start.6 = (f32[2,64,768]{2,1,0:T(8,128)}, f32[2,64,768]{2,1,0:T(8,128)S(1)}, u32[]{:S(2)}) copy-start(f32[2,64,768]{2,1,0:T(8,128)S(1)} %get-tuple-element.395) | copy-start | bytes 1179652
  351.7 41.8 %copy-start.28 = (bf16[512,768]{1,0:T(8,128)(2,1)}, bf16[512,768]{1,0:T(8,128)(2,1)S(1)}, u32[]{:S(2)}) copy-start(bf16[512,768]{1,0:T(8,128)(2,1)S(1)} %get-tuple-element.416) | copy-start | bytes 2359300
  393.5 69.9 %reduce-scatter.23.cloned.1.call-start = ((), (), s32[]{:S(2)}) async-start(), calls=%async_computation.14 | async-start | bytes 1966080 | tf_op jit(solution)/shard_map/reduce_scatter | solution.py:219
  434.8 28.7 %copy-start.51 = (f32[768]{0:T(1024)S(1)}, f32[768]{0:T(1024)}, u32[]{:S(2)}) copy-start(f32[768]{0:T(1024)} %param.41) | copy-start | bytes 9220
  434.8 28.7 %copy-start.54 = (f32[2,64]{1,0:T(2,128)S(1)}, f32[2,64]{1,0:T(2,128)}, u32[]{:S(2)}) copy-start(f32[2,64]{1,0:T(2,128)} %copy-done.52) | copy-start | bytes 1540
  434.8 131.8 %all-reduce.5.cloned.1.call-start = ((), (), s32[]{:S(2)}) async-start(), calls=%async_computation.15 | async-start | bytes 3145728 | tf_op jit(solution)/shard_map/psum | solution.py:244
  496.2 161.4 %reduce-scatter.37.cloned.1.call-start = ((), (), s32[]{:S(2)}) async-start(), calls=%async_computation.22 | async-start | bytes 884736
  531.0 37.0 %copy-start.33 = (bf16[2,256,3,64]{1,3,2,0:T(8,128)(2,1)}, bf16[2,256,3,64]{1,3,2,0:T(8,128)(2,1)S(1)}, u32[]{:S(2)}) copy-start(bf16[2,256,3,64]{1,3,2,0:T(8,128)(2,1)S(1)} %fusion.96) | copy-start | bytes 589828
  532.6 35.4 %copy-start.9 = (bf16[2,256,3,64]{1,3,2,0:T(8,128)(2,1)S(1)}, bf16[2,256,3,64]{1,3,2,0:T(8,128)(2,1)}, u32[]{:S(2)}) copy-start(bf16[2,256,3,64]{1,3,2,0:T(8,128)(2,1)} %get-tuple-element.797) | copy-start | bytes 589828
  532.7 126.6 %reduce-scatter.25.cloned.1.call-start = ((), (), s32[]{:S(2)}) async-start(), calls=%async_computation.16 | async-start | bytes 983040 | tf_op jit(solution)/shard_map/reduce_scatter | solution.py:270
  603.6 121.3 %reduce-scatter.31.cloned.1.call-start = ((), (), s32[]{:S(2)}) async-start(), calls=%async_computation.19 | async-start | bytes 884736
  605.4 192.4 %reduce-scatter.29.cloned.1.call-start = ((), (), s32[]{:S(2)}) async-start(), calls=%async_computation.18 | async-start | bytes 2654208 | tf_op jit(solution)/shard_map/reduce_scatter | solution.py:291
  607.8 263.2 %reduce-scatter.27.cloned.1.call-start = ((), (), s32[]{:S(2)}) async-start(), calls=%async_computation.17 | async-start | bytes 2654208 | tf_op jit(solution)/shard_map/reduce_scatter | solution.py:289
  611.4 325.8 %reduce-scatter.33.cloned.1.call-start = ((), (), s32[]{:S(2)}) async-start(), calls=%async_computation.20 | async-start | bytes 884736
  613.8 389.6 %reduce-scatter.35.cloned.1.call-start = ((), (), s32[]{:S(2)}) async-start(), calls=%async_computation.21 | async-start | bytes 884736
  614.5 44.8 %copy-start.7 = (f32[2,64,768]{2,1,0:T(8,128)S(1)}, f32[2,64,768]{2,1,0:T(8,128)}, u32[]{:S(2)}) copy-start(f32[2,64,768]{2,1,0:T(8,128)} %copy-done.6) | copy-start | bytes 1179652
  614.5 44.8 %copy-start.21 = (f32[2,64,768]{2,1,0:T(8,128)S(1)}, f32[2,64,768]{2,1,0:T(8,128)}, u32[]{:S(2)}) copy-start(f32[2,64,768]{2,1,0:T(8,128)} %copy-done.20) | copy-start | bytes 1179652
  614.5 44.8 %copy-start.55 = (f32[2,64]{1,0:T(2,128)S(1)}, f32[2,64]{1,0:T(2,128)}, u32[]{:S(2)}) copy-start(f32[2,64]{1,0:T(2,128)} %copy-done.52) | copy-start | bytes 1540
  614.5 44.8 %copy-start.75 = (f32[2,64]{1,0:T(2,128)S(1)}, f32[2,64]{1,0:T(2,128)}, u32[]{:S(2)}) copy-start(f32[2,64]{1,0:T(2,128)} %copy-done.74) | copy-start | bytes 1540
  614.5 44.8 %copy-start.77 = (f32[2,64]{1,0:T(2,128)S(1)}, f32[2,64]{1,0:T(2,128)}, u32[]{:S(2)}) copy-start(f32[2,64]{1,0:T(2,128)} %copy-done.76) | copy-start | bytes 1540
  (71 other events, 564.9 us)
Sparse Core Ops, SparseCore 0:
  304.3 28.2 reduce-scatter.18
  393.7 26.3 reduce-scatter.20
  434.9 28.5 reduce-scatter.22
Sparse Core Ops, SparseCore 1:
  306.7 41.7 all-gather.2
  350.4 39.7 all-gather.4
  496.3 70.3 all-reduce.4
  570.0 62.5 reduce-scatter.36
  635.1 22.6 reduce-scatter.24
  661.7 63.1 reduce-scatter.30
  728.8 69.0 reduce-scatter.28
  801.8 69.1 reduce-scatter.26
  874.7 62.4 reduce-scatter.32
  941.1 62.3 reduce-scatter.34
where the time goes:
time: 1020 us; the launch traced here: 1010 us
  waiting for transfers between devices  501 us (49%)
  blocking collectives  320 us (31%)
  local copies, waits for them, and re-layouts  85.6 us (8%)
  matrix products  73.7 us (7%)
  between operations  16.4 us (2%)
  other arithmetic  13 us (1%)
    unnamed x17, waiting for transfers between devices  197 us
    psum x1, blocking collectives, per_device(): kv_sum, z_sum = lax.psum((kv_part, z_part), 'ctx')  96.4 us
    reduce_scatter x1, waiting for transfers between devices, per_device(): lax.psum_scatter(grad_up, ('shard', 'ctx'), scatter_dimension=0, tiled=True)  73.1 us
    reduce_scatter x1, waiting for transfers between devices, per_device(): lax.psum_scatter(grad_down, ('shard', 'ctx'), scatter_dimension=1, tiled=...  73 us
    mul x40, local copies, waits for them, and re-layouts, spread_rows(): wide = mask_low[:, None, :, None] * left[:, :, None, :]  51.8 us
    psum x1, blocking collectives, per_device(): lax.psum((grad_gain_attn, grad_shift_attn, grad_gain_ffn, grad_shift_ffn,...  40.8 us
    all_gather x1, waiting for transfers between devices, per_device(): lax.all_gather(w_down, ('shard', 'ctx'), axis=1, tiled=True)  38.5 us
    psum x1, waiting for transfers between devices, per_device(): lax.psum(kv_grad_part.astype(jnp.bfloat16), 'ctx').astype(jnp.float32)  33.9 us
  transfers between devices with their start and end apart: 13, of which 11 were waited for; matrix products, arithmetic and copies ran while one was open for 7% of the time, Pallas kernels for 0%

commit v1 on v0

--- a/solution.py
+++ b/solution.py
@@ -241,7 +241,9 @@
         "scg,schm->shgm", mask_full, phq_wide * grad_denom[..., None], precision=highest
     )
     kv_grad, z_grad = (
-        lax.psum(kv_grad_part.astype(jnp.bfloat16), "ctx").astype(jnp.float32),
+        jnp.sum(lax.all_gather(kv_grad_part.astype(jnp.bfloat16), "ctx"), axis=0).astype(
+            jnp.float32
+        ),
         lax.psum(z_grad_part.astype(jnp.bfloat16), "ctx").astype(jnp.float32),
     )
     kv_grad_low = kv_grad.astype(jnp.bfloat16)

time: 1020 us -> 1080 us (1.059)
  waiting for transfers between devices: 501 us -> 542 us
    all_gather x0 -> x1, waiting for transfers between devices: none -> 76.6 us  [per_device(): lax.all_gather(kv_grad_part.astype(jnp.bfloat16), 'ctx')]
    psum x1 -> x0, waiting for transfers between devices: 33.9 us -> none  [per_device(): lax.psum(kv_grad_part.astype(jnp.bfloat16), 'ctx').astype(jnp.float32)]
where the time goes in v1:
time: 1080 us; the launch traced here: 1070 us
  waiting for transfers between devices  542 us (50%)
  blocking collectives  330 us (31%)
  local copies, waits for them, and re-layouts  87.8 us (8%)
  matrix products  72.9 us (7%)
  other arithmetic  17.2 us (2%)
  between operations  16.5 us (2%)
    unnamed x17, waiting for transfers between devices  193 us
    psum x1, blocking collectives, per_device(): kv_sum, z_sum = lax.psum((kv_part, z_part), 'ctx')  96.3 us
    all_gather x1, waiting for transfers between devices, per_device(): lax.all_gather(kv_grad_part.astype(jnp.bfloat16), 'ctx')  76.6 us
    reduce_scatter x1, waiting for transfers between devices, per_device(): lax.psum_scatter(grad_up, ('shard', 'ctx'), scatter_dimension=0, tiled=True)  73.1 us
    reduce_scatter x1, waiting for transfers between devices, per_device(): lax.psum_scatter(grad_down, ('shard', 'ctx'), scatter_dimension=1, tiled=...  73 us
    mul x40, local copies, waits for them, and re-layouts, spread_rows(): wide = mask_low[:, None, :, None] * left[:, :, None, :]  51.5 us
    all_gather x1, blocking collectives, per_device(): lax.all_gather(w_out, ('shard', 'ctx'), axis=1, tiled=True)  42.5 us
    psum x1, blocking collectives, per_device(): lax.psum((grad_gain_attn, grad_shift_attn, grad_gain_ffn, grad_shift_ffn,...  39.9 us
  transfers between devices with their start and end apart: 13, of which 11 were waited for; matrix products, arithmetic and copies ran while one was open for 7% of the time, Pallas kernels for 0%

profile of v1, /device:TPU:0, one launch (start us, length us, event | category | flops | bytes accessed | tf_op | source)
XLA Modules:
  0.0 1067.1 jit_solution(2830118090305462046)
XLA Ops:
  8.1 10.4 all_gather.42
  18.5 32.5 %all_gather.43 = bf16[768,192]{1,0:T(8,128)(2,1)S(1)} all-gather(bf16[96,192]{1,0:T(8,128)(2,1)} %param.32), channel_id=1, replica_groups=mesh['shard'=2,'ctx'=4,'tp'=4] {'shard','ctx'}, dimensions={0}, use_global_device_ids=true | all-gather | bytes 331776 | tf_op jit(solution)/shard_map/all_gather | solution.py:122
  56.2 31.6 %all_gather.44 = bf16[768,192]{1,0:T(8,128)(2,1)S(1)} all-gather(bf16[96,192]{1,0:T(8,128)(2,1)S(1)} %copy-done.51), channel_id=1, replica_groups=mesh['shard'=2,'ctx'=4,'tp'=4] {'shard','ctx'}, dimensions={0}, use_global_device_ids=true | all-gather | bytes 331776 | tf_op jit(solution)/shard_map/all_gather | solution.py:123
  92.7 20.7 %while.66 = (s32[]{:T(128)}, f32[2,3,2048,64]{2,3,1,0:T(8,128)}, bf16[2,256,8]{2,1,0:T(8,128)(2,1)S(1)}, bf16[2,256,3,256]{3,1,2,0:T(8,128)(2,1)}, bf16[2,256,3,64]{1,3,2,0:T(8,128)(2,1)}) while((s32[]{:T(128)}, f32[2,3,2048,64]{2,3,1,0:T(8,128)}, bf16[2,256,8]{2,1,0:T(8,128)(2,1)S(1)}, bf16[2,256,3,256]{3,1,2,0:T(8,128)(2,1)}, ...), condition=%wide.region_3.4_spmd.clone, body=%wide.region_2.3_spmd.sunk.clone | while | flops 207618048 | bytes 20427872 | solution.py:151
  95.8 4.2 mul.740
  106.2 4.2 mul.740
  113.4 31.9 %all_gather.45 = bf16[768,192]{1,0:T(8,128)(2,1)S(1)} all-gather(bf16[96,192]{1,0:T(8,128)(2,1)S(1)} %copy-done.52), channel_id=1, replica_groups=mesh['shard'=2,'ctx'=4,'tp'=4] {'shard','ctx'}, dimensions={0}, use_global_device_ids=true | all-gather | bytes 331776 | tf_op jit(solution)/shard_map/all_gather | solution.py:121
  151.9 96.3 %all-reduce.3 = (bf16[2,3,2048,64]{2,3,1,0:T(8,128)(2,1)}, f32[2,3,8,256]{3,2,1,0:T(8,128)S(1)}) all-reduce(f32[2,3,2048,64]{2,3,1,0:T(8,128)} %get-tuple-element.176, f32[2,3,8,256]{3,2,1,0:T(8,128)S(1)} %copy-done.49), channel_id=1, replica_groups=mesh['shard'=2,'ctx'=4,'tp'=4] {'ctx'}, use_global_device_ids=true, to_apply=%region_4.5 | all-reduce | flops 798720 | bytes 4816896 | tf_op jit(solution)/shard_map/psum | solution.py:153
  248.3 19.3 %while.67 = (s32[]{:T(128)}, f32[2,256,3,64]{1,3,2,0:T(8,128)}, bf16[2,3,2048,64]{2,3,1,0:T(8,128)(2,1)}, bf16[2,256,8]{2,1,0:T(8,128)(2,1)S(1)}, bf16[2,256,3,256]{3,1,2,0:T(8,128)(2,1)}) while((s32[]{:T(128)}, f32[2,256,3,64]{1,3,2,0:T(8,128)}, bf16[2,3,2048,64]{2,3,1,0:T(8,128)(2,1)}, bf16[2,256,8]{2,1,0:T(8,128)(2,1)S(1)}, ...), condition=%wide.region_6.7_spmd.clone, body=%wide.region_5.6_spmd.sunk.clone | while | flops 202899456 | bytes 31536224 | solution.py:155
  268.5 42.5 %all_gather.46 = bf16[192,768]{0,1:T(8,128)(2,1)S(1)} all-gather(bf16[192,96]{0,1:T(8,128)(2,1)S(1)} %copy.105), channel_id=1, replica_groups=mesh['shard'=2,'ctx'=4,'tp'=4] {'shard','ctx'}, dimensions={1}, use_global_device_ids=true | all-gather | bytes 331776 | tf_op jit(solution)/shard_map/all_gather | solution.py:125
  315.8 27.3 %reduce-scatter.19.cloned.1.call-done = f32[64,2,768]{2,0,1:T(8,128)} async-done(((f32[256,2,768]{2,0,1:T(8,128)}), f32[64,2,768]{2,0,1:T(8,128)}) %reduce-scatter.19.cloned.1.call-update) | async-done | bytes 393232 | tf_op jit(solution)/shard_map/reduce_scatter | solution.py:166
  344.7 8.0 all_gather.47
  352.7 6.3 all-gather.5.cloned.1.call-done
  362.4 38.4 %all-gather.7.cloned.1.call-done = bf16[768,768]{0,1:T(8,128)(2,1)} async-done(((bf16[768,96]{0,1:T(8,128)(2,1)}), bf16[768,768]{0,1:T(8,128)(2,1)}) %all-gather.7.cloned.1.call-update) | async-done | bytes 1179664 | tf_op jit(solution)/shard_map/all_gather | solution.py:126
  404.1 26.5 %reduce-scatter.21.cloned.1.call-done = f32[64,2,768]{2,0,1:T(8,128)} async-done(((f32[256,2,768]{2,0,1:T(8,128)}), f32[64,2,768]{2,0,1:T(8,128)}) %reduce-scatter.21.cloned.1.call-update) | async-done | bytes 393232 | tf_op jit(solution)/shard_map/reduce_scatter | solution.py:187
  432.5 8.1 all_gather.50
  446.9 27.1 %reduce-scatter.23.cloned.1.call-done = f32[64,2,768]{2,0,1:T(8,128)} async-done(((f32[256,2,768]{2,0,1:T(8,128)}), f32[64,2,768]{2,0,1:T(8,128)}) %reduce-scatter.23.cloned.1.call-update) | async-done | bytes 393232 | tf_op jit(solution)/shard_map/reduce_scatter | solution.py:219
  476.9 8.0 all_gather.51
  486.6 20.1 %while.69 = (s32[]{:T(128)}, bf16[2,3,2048,64]{2,3,1,0:T(8,128)(2,1)}, bf16[2,256,8]{2,1,0:T(8,128)(2,1)S(1)}, bf16[2,256,3,256]{3,1,2,0:T(8,128)(2,1)}, bf16[2,256,3,64]{1,3,2,0:T(8,128)(2,1)}) while((s32[]{:T(128)}, bf16[2,3,2048,64]{2,3,1,0:T(8,128)(2,1)}, bf16[2,256,8]{2,1,0:T(8,128)(2,1)S(1)}, ...), condition=%wide.region_26.27_spmd.clone, body=%wide.region_25.26_spmd.sunk.clone | while | flops 207618048 | bytes 20427872 | solution.py:239
  489.8 4.2 mul.752
  499.8 4.2 mul.752
  511.1 7.0 while.68
  521.8 20.7 %psum.65 = bf16[2,3,8,256]{3,2,1,0:T(8,128)(2,1)S(1)} all-reduce(bf16[2,3,8,256]{3,2,1,0:T(8,128)(2,1)S(1)} %fusion.107), channel_id=1, replica_groups=mesh['shard'=2,'ctx'=4,'tp'=4] {'ctx'}, use_global_device_ids=true, to_apply=%region_31.32 | all-reduce | flops 12288 | bytes 49152 | tf_op jit(solution)/shard_map/psum | solution.py:247
  546.9 76.6 %all-gather.9.cloned.1.call-done = bf16[8,3,2048,64]{2,3,1,0:T(8,128)(2,1)} async-done(((bf16[2,3,2048,64]{2,3,1,0:T(8,128)(2,1)}), bf16[8,3,2048,64]{2,3,1,0:T(8,128)(2,1)}) %all-gather.9.cloned.1.call-update) | async-done | bytes 6291472 | tf_op jit(solution)/shard_map/all_gather | solution.py:244
  629.1 5.1 while.70
  639.5 22.2 %while.71 = (s32[]{:T(128)}, bf16[2,256,3,64]{1,3,2,0:T(8,128)(2,1)}, bf16[2,3,2048,64]{2,3,1,0:T(8,128)(2,1)S(1)}, bf16[2,256,8]{2,1,0:T(8,128)(2,1)S(1)}, bf16[2,256,3,256]{3,1,2,0:T(8,128)(2,1)}) while((s32[]{:T(128)}, bf16[2,256,3,64]{1,3,2,0:T(8,128)(2,1)}, bf16[2,3,2048,64]{2,3,1,0:T(8,128)(2,1)S(1)}, ...), condition=%wide.region_34.35_spmd.clone, body=%wide.region_33.34_spmd.sunk.clone | while | flops 202899456 | bytes 45692112 | solution.py:256
  677.5 39.9 %all-reduce = (f32[768]{0:T(1024)}, f32[768]{0:T(1024)}, f32[3072]{0:T(1024)S(1)}, f32[768]{0:T(1024)}, f32[768]{0:T(1024)}, /*index=5*/f32[768]{0:T(1024)}) all-reduce(f32[768]{0:T(1024)S(1)} %copy-done.64, f32[768]{0:T(1024)S(1)} %copy-done.63, ...), channel_id=1, replica_groups=mesh['shard'=2,'ctx'=4,'tp'=4] {'shard','ctx','tp'}, use_global_device_ids=true, to_apply=%region_41.42 | all-reduce | flops 6912 | bytes 55296 | tf_op jit(solution)/shard_map/psum | solution.py:300
  721.6 59.2 %reduce-scatter.31.cloned.1.call-done = f32[96,192]{1,0:T(8,128)} async-done(((f32[768,192]{1,0:T(8,128)}), f32[96,192]{1,0:T(8,128)}) %reduce-scatter.31.cloned.1.call-update) | async-done | bytes 73744
  780.8 73.0 %reduce-scatter.29.cloned.1.call-done = f32[768,96]{0,1:T(8,128)} async-done(((f32[768,768]{0,1:T(8,128)}), f32[768,96]{0,1:T(8,128)}) %reduce-scatter.29.cloned.1.call-update) | async-done | bytes 294928 | tf_op jit(solution)/shard_map/reduce_scatter | solution.py:293
  853.8 73.1 %reduce-scatter.27.cloned.1.call-done = f32[96,768]{1,0:T(8,128)} async-done(((f32[768,768]{1,0:T(8,128)}), f32[96,768]{1,0:T(8,128)}) %reduce-scatter.27.cloned.1.call-update) | async-done | bytes 294928 | tf_op jit(solution)/shard_map/reduce_scatter | solution.py:291
  926.9 66.5 %reduce-scatter.33.cloned.1.call-done = f32[96,192]{1,0:T(8,128)} async-done(((f32[768,192]{1,0:T(8,128)}), f32[96,192]{1,0:T(8,128)}) %reduce-scatter.33.cloned.1.call-update) | async-done | bytes 73744
  993.4 66.3 %reduce-scatter.35.cloned.1.call-done = f32[96,192]{1,0:T(8,128)} async-done(((f32[768,192]{1,0:T(8,128)}), f32[96,192]{1,0:T(8,128)}) %reduce-scatter.35.cloned.1.call-update) | async-done | bytes 73744
  (349 shorter events, 163.1 us)
Async XLA Ops:
  8.0 44.3 %copy-start = (f32[3,64,256]{2,1,0:T(8,128)S(1)}, f32[3,64,256]{2,1,0:T(8,128)}, u32[]{:S(2)}) copy-start(f32[3,64,256]{2,1,0:T(8,128)} %param.30) | copy-start | bytes 589828
  8.0 335.1 %reduce-scatter.19.cloned.1.call-start = ((), (), s32[]{:S(2)}) async-start(), calls=%async_computation.10 | async-start | bytes 1966080 | tf_op jit(solution)/shard_map/reduce_scatter | solution.py:166
  18.5 69.3 %copy-start.6 = (bf16[2,256,768]{2,1,0:T(8,128)(2,1)}, bf16[2,256,768]{2,1,0:T(8,128)(2,1)S(1)}, u32[]{:S(2)}) copy-start(bf16[2,256,768]{2,1,0:T(8,128)(2,1)S(1)} %all_gather.42) | copy-start | bytes 2359300
  56.2 33.5 %copy-start.56 = (s32[2,256]{1,0:T(2,128)S(1)}, s32[2,256]{1,0:T(2,128)}, u32[]{:S(2)}) copy-start(s32[2,256]{1,0:T(2,128)} %param.29) | copy-start | bytes 6148
  150.7 97.6 %copy-start.25 = (bf16[2,256,3,256]{1,3,0,2:T(8,128)(2,1)}, bf16[2,256,3,256]{1,3,0,2:T(8,128)(2,1)S(1)}, u32[]{:S(2)}) copy-start(bf16[2,256,3,256]{1,3,0,2:T(8,128)(2,1)S(1)} %get-tuple-element.414) | copy-start | bytes 2359300
  267.6 45.3 %copy-start.48 = (f32[2,256,3,64]{1,3,2,0:T(8,128)S(1)}, f32[2,256,3,64]{1,3,2,0:T(8,128)}, u32[]{:S(2)}) copy-start(f32[2,256,3,64]{1,3,2,0:T(8,128)} %get-tuple-element.177) | copy-start | bytes 1179652
  312.9 30.2 %copy-start.45 = (bf16[2,64,768]{2,1,0:T(8,128)(2,1)S(1)}, bf16[2,64,768]{2,1,0:T(8,128)(2,1)}, u32[]{:S(2)}) copy-start(bf16[2,64,768]{2,1,0:T(8,128)(2,1)} %param.28) | copy-start | bytes 589828
  314.6 29.9 %copy-start.50 = (f32[768]{0:T(1024)S(1)}, f32[768]{0:T(1024)}, u32[]{:S(2)}) copy-start(f32[768]{0:T(1024)} %param.35) | copy-start | bytes 9220
  314.6 29.9 %copy-start.59 = (f32[768]{0:T(1024)S(1)}, f32[768]{0:T(1024)}, u32[]{:S(2)}) copy-start(f32[768]{0:T(1024)} %param.36) | copy-start | bytes 9220
  314.6 44.4 %all-gather.5.cloned.1.call-start = ((), (), s32[]{:S(2)}) async-start(), calls=%async_computation.11 | async-start | bytes 1327104 | tf_op jit(solution)/shard_map/all_gather | solution.py:124
  315.2 43.9 %copy-start.75 = (f32[768]{0:T(1024)S(1)}, f32[768]{0:T(1024)}, u32[]{:S(2)}) copy-start(f32[768]{0:T(1024)} %param.38) | copy-start | bytes 9220
  315.2 85.6 %all-gather.7.cloned.1.call-start = ((), (), s32[]{:S(2)}) async-start(), calls=%async_computation.12 | async-start | bytes 1327104 | tf_op jit(solution)/shard_map/all_gather | solution.py:126
  315.8 114.8 %reduce-scatter.21.cloned.1.call-start = ((), (), s32[]{:S(2)}) async-start(), calls=%async_computation.13 | async-start | bytes 1966080 | tf_op jit(solution)/shard_map/reduce_scatter | solution.py:187
  344.3 132.4 %copy-start.8 = (f32[2,64,768]{2,1,0:T(8,128)}, f32[2,64,768]{2,1,0:T(8,128)S(1)}, u32[]{:S(2)}) copy-start(f32[2,64,768]{2,1,0:T(8,128)S(1)} %get-tuple-element.395) | copy-start | bytes 1179652
  344.5 132.2 %copy-start.54 = (f32[2,64]{1,0:T(2,128)}, f32[2,64]{1,0:T(2,128)S(1)}, u32[]{:S(2)}) copy-start(f32[2,64]{1,0:T(2,128)S(1)} %add_rsqrt_fusion.1) | copy-start | bytes 1540
  362.4 41.7 %copy-start.29 = (bf16[512,768]{1,0:T(8,128)(2,1)}, bf16[512,768]{1,0:T(8,128)(2,1)S(1)}, u32[]{:S(2)}) copy-start(bf16[512,768]{1,0:T(8,128)(2,1)S(1)} %get-tuple-element.416) | copy-start | bytes 2359300
  404.1 69.9 %reduce-scatter.23.cloned.1.call-start = ((), (), s32[]{:S(2)}) async-start(), calls=%async_computation.14 | async-start | bytes 1966080 | tf_op jit(solution)/shard_map/reduce_scatter | solution.py:219
  445.3 28.7 %copy-start.71 = (f32[768]{0:T(1024)S(1)}, f32[768]{0:T(1024)}, u32[]{:S(2)}) copy-start(f32[768]{0:T(1024)} %param.42) | copy-start | bytes 9220
  445.3 178.3 %all-gather.9.cloned.1.call-start = ((), (), s32[]{:S(2)}) async-start(), calls=%async_computation.18 | async-start | bytes 7864320 | tf_op jit(solution)/shard_map/all_gather | solution.py:244
  506.8 211.3 %reduce-scatter.37.cloned.1.call-start = ((), (), s32[]{:S(2)}) async-start(), calls=%async_computation.22 | async-start | bytes 884736
  545.0 82.8 %copy-start.34 = (bf16[2,256,3,64]{1,3,2,0:T(8,128)(2,1)}, bf16[2,256,3,64]{1,3,2,0:T(8,128)(2,1)S(1)}, u32[]{:S(2)}) copy-start(bf16[2,256,3,64]{1,3,2,0:T(8,128)(2,1)S(1)} %fusion.96) | copy-start | bytes 589828
  546.7 173.0 %reduce-scatter.25.cloned.1.call-start = ((), (), s32[]{:S(2)}) async-start(), calls=%async_computation.15 | async-start | bytes 983040 | tf_op jit(solution)/shard_map/reduce_scatter | solution.py:272
  665.2 115.6 %reduce-scatter.31.cloned.1.call-start = ((), (), s32[]{:S(2)}) async-start(), calls=%async_computation.19 | async-start | bytes 884736
  666.8 187.0 %reduce-scatter.29.cloned.1.call-start = ((), (), s32[]{:S(2)}) async-start(), calls=%async_computation.17 | async-start | bytes 2654208 | tf_op jit(solution)/shard_map/reduce_scatter | solution.py:293
  669.2 257.7 %reduce-scatter.27.cloned.1.call-start = ((), (), s32[]{:S(2)}) async-start(), calls=%async_computation.16 | async-start | bytes 2654208 | tf_op jit(solution)/shard_map/reduce_scatter | solution.py:291
  672.8 320.6 %reduce-scatter.33.cloned.1.call-start = ((), (), s32[]{:S(2)}) async-start(), calls=%async_computation.20 | async-start | bytes 884736
  675.2 384.4 %reduce-scatter.35.cloned.1.call-start = ((), (), s32[]{:S(2)}) async-start(), calls=%async_computation.21 | async-start | bytes 884736
  675.9 43.8 %copy-start.9 = (f32[2,64,768]{2,1,0:T(8,128)S(1)}, f32[2,64,768]{2,1,0:T(8,128)}, u32[]{:S(2)}) copy-start(f32[2,64,768]{2,1,0:T(8,128)} %copy-done.8) | copy-start | bytes 1179652
  675.9 43.8 %copy-start.22 = (f32[2,64,768]{2,1,0:T(8,128)S(1)}, f32[2,64,768]{2,1,0:T(8,128)}, u32[]{:S(2)}) copy-start(f32[2,64,768]{2,1,0:T(8,128)} %copy-done.21) | copy-start | bytes 1179652
  676.0 43.8 %copy-start.55 = (f32[2,64]{1,0:T(2,128)S(1)}, f32[2,64]{1,0:T(2,128)}, u32[]{:S(2)}) copy-start(f32[2,64]{1,0:T(2,128)} %copy-done.54) | copy-start | bytes 1540
  676.0 43.8 %copy-start.66 = (f32[2,64]{1,0:T(2,128)S(1)}, f32[2,64]{1,0:T(2,128)}, u32[]{:S(2)}) copy-start(f32[2,64]{1,0:T(2,128)} %copy-done.65) | copy-start | bytes 1540
  676.0 43.8 %copy-start.68 = (f32[2,64]{1,0:T(2,128)S(1)}, f32[2,64]{1,0:T(2,128)}, u32[]{:S(2)}) copy-start(f32[2,64]{1,0:T(2,128)} %copy-done.67) | copy-start | bytes 1540
  (66 other events, 340.8 us)
Sparse Core Ops, SparseCore 0:
  314.7 28.4 reduce-scatter.18
  404.2 26.3 reduce-scatter.20
  445.4 28.5 reduce-scatter.22
Sparse Core Ops, SparseCore 1:
  317.2 41.8 all-gather.4
  361.0 39.7 all-gather.6
  506.8 116.7 all-gather.8
  626.9 61.6 reduce-scatter.36
  691.1 22.2 reduce-scatter.24
  717.3 63.4 reduce-scatter.30
  784.7 69.0 reduce-scatter.28
  857.7 69.1 reduce-scatter.26
  930.7 62.7 reduce-scatter.32
  997.3 62.3 reduce-scatter.34
